TPU v7x, 512 devices: a whole 4x4x16 slice. The times are simulated.
512 devices in a mesh: dp: 16 (over z), expert: 32 (over y, x, core).
Axes of the slice: x: 4, y: 4, z: 16, core: 2. Of those that a mesh axis runs over, the one named last changes fastest.
Arguments:
- tokens: bfloat16 [4096, 4096], P('expert', 'dp'), may hold values from -6 to 6
- routing: int32 [4096, 8], P('expert'), may hold values from 0 to 31, all different within a row; in each aligned block of 128 rows (0 to 127, 128 to 255, ...) at most 40 rows name the same one
- gate_probs: float32 [4096, 8], P('expert'), may hold values from 0.05 to 0.3
- paired: int32 [32], P('expert'), may hold values from 0 to 1, as said below
- w_gate: bfloat16 [32, 4096, 768], P('expert', 'dp'), may hold values from -0.09375 to 0.09375
- w_up: bfloat16 [32, 4096, 768], P('expert', 'dp'), may hold values from -0.09375 to 0.09375
- w_down: bfloat16 [32, 768, 4096], P('expert', None, 'dp'), may hold values from -0.21875 to 0.21875
- cotangent: bfloat16 [4096, 4096], P('expert', 'dp'), may hold values from -6 to 6
Outputs:
- output: bfloat16 [4096, 4096], P('expert', 'dp')
- grad_tokens: bfloat16 [4096, 4096], P('expert', 'dp')
- grad_gate: float32 [32, 4096, 768], P('expert', 'dp')
- grad_up: float32 [32, 4096, 768], P('expert', 'dp')
- grad_down: float32 [32, 768, 4096], P('expert', None, 'dp')
Inputs may be any that keep to these rules, and one draw needn't show every extreme that they name: `routing`: each token names 8 different copies; among the tokens of one source (aligned blocks of 128 tokens) no copy is named more than 40 times, a bound that some block reaches. paired[c] equals paired[(c + 16) mod 32]; paired[0] and paired[31] are 1.
All inputs are finite; a program needn't handle non-finite values.
Results may differ from a plain program's by a relative error of at most 0.029.
Values may be sent and summed in bfloat16 or wider, within the bound.
A program may use at most 64 MiB of HBM per device.

v0:
```python
import jax
import jax.numpy as jnp
from jax import lax
from jax.sharding import PartitionSpec as P


def swapped(value, axis, stride):
    mask = 2**stride
    pairs = [(source, source ^ mask) for source in range(lax.axis_size(axis))]
    return lax.ppermute(value, axis, pairs)


def product(left, right):
    return jnp.dot(left, right, preferred_element_type=jnp.float32)


def inner_rows(left, right):
    return lax.dot_general(
        left, right, (((0,), (0,)), ((), ())), preferred_element_type=jnp.float32
    )


def outer_cols(left, right):
    return lax.dot_general(
        left, right, (((1,), (1,)), ((), ())), preferred_element_type=jnp.float32
    )


def rounded(value):
    return lax.optimization_barrier(value.astype(jnp.bfloat16)).astype(jnp.float32)


def per_device(tokens, routing, gate_probs, paired, w_gate, w_up, w_down, cotangent):
    n_expert = lax.axis_size("expert")
    n_data = lax.axis_size("dp")
    token_count, top_count = routing.shape
    slab = tokens.shape[1]
    hidden = w_gate.shape[2]
    capacity = max(2, 5 * token_count * top_count // (4 * n_expert))
    all_rows = n_expert * capacity
    own_rows = all_rows // n_data
    gate_slab = w_gate[0]
    up_slab = w_up[0]
    down_slab = w_down[0]
    flat_route = routing.reshape(token_count * top_count)
    onehot = (flat_route[:, None] == jnp.arange(n_expert, dtype=jnp.int32)[None, :]).astype(
        jnp.int32
    )
    earlier = jnp.cumsum(onehot, axis=0) - onehot
    target = flat_route * capacity + jnp.sum(earlier * onehot, axis=1)
    select = jnp.arange(all_rows, dtype=jnp.int32)[:, None] == target[None, :]
    select_grid = select.reshape(all_rows, token_count, top_count)
    token_select = jnp.any(select_grid, axis=2).astype(jnp.bfloat16)
    weight_select = jnp.sum(select_grid.astype(jnp.float32) * gate_probs[None, :, :], axis=2)
    weight_high = weight_select.astype(jnp.bfloat16)
    weight_low = (weight_select - weight_high.astype(jnp.float32)).astype(jnp.bfloat16)
    send_tokens = product(token_select, tokens).astype(jnp.bfloat16)
    scaled = (gate_probs[:, :, None] * cotangent.astype(jnp.float32)[:, None, :]).astype(
        jnp.bfloat16
    )
    send_grads = product(
        select.astype(jnp.bfloat16), scaled.reshape(token_count * top_count, slab)
    ).astype(jnp.bfloat16)
    arrived = (
        lax.all_to_all(
            send_tokens.reshape(n_expert, capacity, slab),
            "expert",
            split_axis=0,
            concat_axis=0,
            tiled=True,
        ),
        lax.all_to_all(
            send_grads.reshape(n_expert, capacity, slab),
            "expert",
            split_axis=0,
            concat_axis=0,
            tiled=True,
        ),
    )
    token_slab = arrived[0].reshape(all_rows, slab)
    grad_slab = arrived[1].reshape(all_rows, slab)
    block_rows = token_slab
    summed = lax.psum_scatter(
        rounded(
            jnp.concatenate([product(block_rows, gate_slab), product(block_rows, up_slab)], axis=1)
        ).astype(jnp.bfloat16),
        "dp",
        scatter_dimension=0,
        tiled=True,
    ).astype(jnp.float32)
    gate_own = summed[:, :hidden]
    up_own = summed[:, hidden:]
    hid_own = (jax.nn.silu(gate_own) * up_own).astype(jnp.bfloat16)
    piece = lax.all_gather(hid_own, "dp", axis=0, tiled=True)
    answer_acc = product(piece, down_slab)
    grad_down = inner_rows(piece, grad_slab)
    answer_slab = answer_acc.astype(jnp.bfloat16)
    answer_back = lax.all_to_all(
        answer_slab.reshape(n_expert, capacity, slab),
        "expert",
        split_axis=0,
        concat_axis=0,
        tiled=True,
    )
    hidden_parts = (
        outer_cols(grad_slab, down_slab).astype(jnp.bfloat16).reshape(n_data, own_rows, hidden)
    )
    arrived_parts = lax.all_to_all(hidden_parts, "dp", split_axis=0, concat_axis=0, tiled=True)
    grad_hidden = jnp.sum(arrived_parts.astype(jnp.float32), axis=0)
    sigma = jax.nn.sigmoid(gate_own)
    activated = gate_own * sigma
    grad_gate_rows = (grad_hidden * up_own * sigma * (1.0 + gate_own * (1.0 - sigma))).astype(
        jnp.bfloat16
    )
    grad_up_rows = (grad_hidden * activated).astype(jnp.bfloat16)
    piece_gate = lax.all_gather(grad_gate_rows, "dp", axis=0, tiled=True)
    piece_up = lax.all_gather(grad_up_rows, "dp", axis=0, tiled=True)
    block_rows = token_slab
    gate_acc = inner_rows(block_rows, piece_gate)
    up_acc = inner_rows(block_rows, piece_up)
    back_rows = outer_cols(piece_gate, gate_slab) + outer_cols(piece_up, up_slab)
    grad_gate = gate_acc
    grad_up = up_acc
    back_slab = back_rows.astype(jnp.bfloat16)
    back_rows_home = lax.all_to_all(
        back_slab.reshape(n_expert, capacity, slab),
        "expert",
        split_axis=0,
        concat_axis=0,
        tiled=True,
    )
    answer_home = answer_back.reshape(all_rows, slab)
    output = (inner_rows(weight_high, answer_home) + inner_rows(weight_low, answer_home)).astype(
        jnp.bfloat16
    )
    grad_tokens = inner_rows(token_select, back_rows_home.reshape(all_rows, slab)).astype(
        jnp.bfloat16
    )
    other = (
        swapped(grad_gate.astype(jnp.bfloat16), "expert", n_expert.bit_length() - 2).astype(
            grad_gate.dtype
        ),
        swapped(grad_up.astype(jnp.bfloat16), "expert", n_expert.bit_length() - 2).astype(
            grad_up.dtype
        ),
        swapped(grad_down.astype(jnp.bfloat16), "expert", n_expert.bit_length() - 2).astype(
            grad_down.dtype
        ),
    )
    keep = paired.astype(jnp.float32)[0]
    grad_gate = (grad_gate + keep * other[0])[None]
    grad_up = (grad_up + keep * other[1])[None]
    grad_down = (grad_down + keep * other[2])[None]
    return (output, grad_tokens, grad_gate, grad_up, grad_down)


def solution(mesh):
    return jax.shard_map(
        per_device,
        mesh=mesh,
        in_specs=(
            P("expert", "dp"),
            P("expert", None),
            P("expert", None),
            P("expert"),
            P("expert", "dp", None),
            P("expert", "dp", None),
            P("expert", None, "dp"),
            P("expert", "dp"),
        ),
        out_specs=(
            P("expert", "dp"),
            P("expert", "dp"),
            P("expert", "dp", None),
            P("expert", "dp", None),
            P("expert", None, "dp"),
        ),
        check_vma=False,
    )
```

profile of v0, /device:TPU:1, one launch (start us, length us, event | category | flops | bytes accessed | tf_op | source)
XLA Modules:
  0.0 480.7 jit_solution(16176602574999856850)
XLA Ops:
  7.2 0.0 copy-start
  7.2 0.8 copy.41
  8.0 0.1 eq.50
  8.1 0.1 eq.46
  8.2 0.0 copy-start.12
  8.2 9.0 %reduce-window.6 = s32[32,8,128]{2,1,0:T(8,128)S(1)} reduce-window(s32[32,8,128]{2,1,0:T(8,128)S(1)} %fusion.24, s32[]{:T(128)} %constant.7.clone.1), window={size=1x1x128 pad=0_0x0_0x127_0}, to_apply=%region_0.0 | reduce-window | flops 4161536 | bytes 262148 | tf_op jit(solution)/shard_map/reduce-window
  17.3 0.1 slice.16
  17.4 0.1 copy.43
  17.5 0.1 copy.44
  17.6 0.1 broadcast_add_fusion
  17.8 0.1 reduce_sum.30
  17.9 0.7 multiply_add_fusion.1
  18.6 4.6 fusion
  23.3 2.1 convolution_convert_fusion.4
  25.3 10.4 %all-to-all-start = ((bf16[32,40,256]{2,1,0:T(8,128)(2,1)}), bf16[32,40,256]{2,1,0:T(8,128)(2,1)S(1)}, u32[]{:S(2)}, u32[]{:S(2)}) async-start(bf16[32,40,256]{2,1,0:T(8,128)(2,1)} %bitcast.2), calls=%async_computation | async-start | bytes 1310720 | tf_op jit(solution)/shard_map/all_to_all | solution.py:65
  35.8 0.1 copy.47
  35.9 0.1 mul.92
  36.0 0.0 copy-start.6
  36.0 1.9 fusion.4
  38.0 10.8 %all-to-all-done = bf16[32,40,256]{2,1,0:T(8,128)(2,1)S(1)} async-done(((bf16[32,40,256]{2,1,0:T(8,128)(2,1)}), bf16[32,40,256]{2,1,0:T(8,128)(2,1)S(1)}, u32[]{:S(2)}, u32[]{:S(2)}) %all-to-all-start) | async-done | bytes 655392 | tf_op jit(solution)/shard_map/all_to_all | solution.py:65
  48.8 4.2 all-to-all-start.2
  53.0 0.0 reduce-scatter.4.cloned.1.call-start
  53.1 0.7 convolution_convert_fusion.1
  53.8 0.7 convolution_convert_fusion.2
  54.5 2.1 pad_maximum_fusion
  56.7 6.3 %copy.48 = bf16[1280,1536]{1,0:T(8,128)(2,1)} copy(bf16[1280,1536]{0,1:T(8,128)(2,1)} %pad_maximum_fusion) | data formatting | bytes 7864320
  63.0 0.0 reduce-scatter.4.cloned.1.call-update
  63.0 0.0 all-gather.4.cloned.1.call-start
  63.0 3.0 all-to-all-done.2
  66.1 0.7 convolution_convert_fusion
  66.8 117.4 %all_to_all.25 = bf16[16,80,768]{2,1,0:T(8,128)(2,1)S(1)} all-to-all(bf16[16,80,768]{2,1,0:T(8,128)(2,1)S(1)} %bitcast.77), channel_id=1, replica_groups=mesh['dp'=16,'expert'=32] {'dp'}, dimensions={0} | all-to-all | bytes 3932160 | tf_op jit(solution)/shard_map/all_to_all | solution.py:108
  184.2 0.3 convert_reduce_fusion
  184.5 27.7 %reduce-scatter.4.cloned.1.call-done = bf16[80,1536]{1,0:T(8,128)(2,1)} async-done(((bf16[1280,1536]{1,0:T(8,128)(2,1)}), bf16[80,1536]{1,0:T(8,128)(2,1)}) %reduce-scatter.4.cloned.1.call-update) | async-done | bytes 245776 | tf_op jit(solution)/shard_map/reduce_scatter | solution.py:83
  212.2 1.0 convert_element_type.90
  213.2 0.9 multiply_convert_fusion
  214.1 0.0 all-gather.4.cloned.1.call-update
  214.1 0.0 all-gather.6.cloned.1.call-start
  214.1 0.7 all-gather.6.cloned.1.call-update
  214.8 0.2 all-gather.8.cloned.1.call-start
  215.1 0.3 all-gather.8.cloned.1.call-update
  216.1 6.8 %select_reduce_fusion = f32[1280,128]{1,0:T(8,128)S(1)} fusion(f32[128,8]{0,1:T(8,128)S(1)} %copy-done.12, s32[128,8]{0,1:T(8,128)S(1)} %multiply_add_fusion.1), kind=kLoop, calls=%fused_computation.1 | loop fusion | flops 3768320 | bytes 663552 | tf_op jit(solution)/shard_map/reduce_sum | solution.py:54
  222.8 56.5 %all-gather.4.cloned.1.call-done = bf16[1280,768]{1,0:T(8,128)(2,1)} async-done(((bf16[80,768]{1,0:T(8,128)(2,1)}), bf16[1280,768]{1,0:T(8,128)(2,1)}) %all-gather.4.cloned.1.call-update) | async-done | bytes 1966096 | tf_op jit(solution)/shard_map/all_gather | solution.py:94
  279.3 3.1 convolution_convert_fusion.3
  282.4 17.4 %all-to-all-start.1 = ((bf16[32,40,256]{2,1,0:T(8,128)(2,1)}), bf16[32,40,256]{2,1,0:T(8,128)(2,1)S(1)}, u32[]{:S(2)}, u32[]{:S(2)}) async-start(bf16[32,40,256]{2,1,0:T(8,128)(2,1)} %bitcast.7), calls=%async_computation.1 | async-start | bytes 1310720 | tf_op jit(solution)/shard_map/all_to_all | solution.py:98
  299.7 52.7 %all-gather.6.cloned.1.call-done = bf16[1280,768]{1,0:T(8,128)(2,1)} async-done(((bf16[80,768]{1,0:T(8,128)(2,1)}), bf16[1280,768]{1,0:T(8,128)(2,1)}) %all-gather.6.cloned.1.call-update) | async-done | bytes 1966096 | tf_op jit(solution)/shard_map/all_gather | solution.py:116
  352.4 3.0 fusion.25
  355.4 4.6 collective-permute-start
  360.1 64.6 %all-gather.8.cloned.1.call-done = bf16[1280,768]{1,0:T(8,128)(2,1)} async-done(((bf16[80,768]{1,0:T(8,128)(2,1)}), bf16[1280,768]{1,0:T(8,128)(2,1)}) %all-gather.8.cloned.1.call-update) | async-done | bytes 1966096 | tf_op jit(solution)/shard_map/all_gather | solution.py:117
  424.7 2.4 fusion.26
  427.1 4.8 collective-permute-start.1
  431.9 1.7 fusion.27
  433.6 2.3 collective-permute-start.2
  435.9 0.7 fusion.14
  436.6 1.6 fusion.3
  438.2 0.0 collective-permute-done
  438.2 2.0 add_bitcast_fusion.2
  440.2 0.0 collective-permute-done.1
  440.2 1.0 add_bitcast_fusion.1
  441.1 18.0 %all-to-all-start.4 = ((bf16[32,40,256]{2,1,0:T(8,128)(2,1)}), bf16[32,40,256]{2,1,0:T(8,128)(2,1)}, u32[]{:S(2)}, u32[]{:S(2)}) async-start(bf16[32,40,256]{2,1,0:T(8,128)(2,1)} %bitcast.13), calls=%async_computation.4 | async-start | bytes 1310720 | tf_op jit(solution)/shard_map/all_to_all | solution.py:125
  459.1 2.0 add_bitcast_fusion
  461.1 0.3 fusion.19
  461.4 0.9 fusion.5
  462.3 9.8 %all-to-all-done.4 = bf16[32,40,256]{2,1,0:T(8,128)(2,1)} async-done(((bf16[32,40,256]{2,1,0:T(8,128)(2,1)}), bf16[32,40,256]{2,1,0:T(8,128)(2,1)}, u32[]{:S(2)}, u32[]{:S(2)}) %all-to-all-start.4) | async-done | bytes 655392 | tf_op jit(solution)/shard_map/all_to_all | solution.py:125
  472.1 2.1 convolution_convert_fusion.5
  (34 shorter events, 0.2 us)
Async XLA Ops:
  7.2 58.9 %copy-start = (bf16[1,768,256]{2,1,0:T(8,128)(2,1)S(1)}, bf16[1,768,256]{2,1,0:T(8,128)(2,1)}, u32[]{:S(2)}) copy-start(bf16[1,768,256]{2,1,0:T(8,128)(2,1)} %param.14) | copy-start | bytes 1179652
  8.0 27.8 %copy-start.11 = (bf16[128,256]{1,0:T(8,128)(2,1)S(1)}, bf16[128,256]{1,0:T(8,128)(2,1)}, u32[]{:S(2)}) copy-start(bf16[128,256]{1,0:T(8,128)(2,1)} %param.15) | copy-start | bytes 196612
  8.2 27.6 %copy-start.12 = (f32[128,8]{0,1:T(8,128)S(1)}, f32[128,8]{0,1:T(8,128)}, u32[]{:S(2)}) copy-start(f32[128,8]{0,1:T(8,128)} %param.10) | copy-start | bytes 12292
  23.3 2.1 copy-start.9
  25.3 23.5 %all-to-all-start = ((bf16[32,40,256]{2,1,0:T(8,128)(2,1)}), bf16[32,40,256]{2,1,0:T(8,128)(2,1)S(1)}, u32[]{:S(2)}, u32[]{:S(2)}) async-start(bf16[32,40,256]{2,1,0:T(8,128)(2,1)} %bitcast.2), calls=%async_computation | async-start | bytes 1310720 | tf_op jit(solution)/shard_map/all_to_all | solution.py:65
  36.0 17.1 %copy-start.6 = (bf16[1,256,768]{2,1,0:T(8,128)(2,1)S(1)}, bf16[1,256,768]{2,1,0:T(8,128)(2,1)}, u32[]{:S(2)}) copy-start(bf16[1,256,768]{2,1,0:T(8,128)(2,1)} %param.13) | copy-start | bytes 1179652
  48.8 5.0 %copy-start.5 = (bf16[1,256,768]{2,1,0:T(8,128)(2,1)S(1)}, bf16[1,256,768]{2,1,0:T(8,128)(2,1)}, u32[]{:S(2)}) copy-start(bf16[1,256,768]{2,1,0:T(8,128)(2,1)} %param.12) | copy-start | bytes 1179652
  48.8 17.3 %all-to-all-start.2 = ((bf16[32,40,256]{2,1,0:T(8,128)(2,1)}), bf16[32,40,256]{2,1,0:T(8,128)(2,1)S(1)}, u32[]{:S(2)}, u32[]{:S(2)}) async-start(bf16[32,40,256]{2,1,0:T(8,128)(2,1)} %bitcast.10), calls=%async_computation.2 | async-start | bytes 1310720 | tf_op jit(solution)/shard_map/all_to_all | solution.py:72
  53.0 159.2 %reduce-scatter.4.cloned.1.call-start = ((), (), s32[]{:S(2)}) async-start(), calls=%async_computation.9 | async-start | bytes 4177920 | tf_op jit(solution)/shard_map/reduce_scatter | solution.py:83
  63.0 216.3 %all-gather.4.cloned.1.call-start = ((), (), s32[]{:S(2)}) async-start(), calls=%async_computation.6 | async-start | bytes 2088960 | tf_op jit(solution)/shard_map/all_gather | solution.py:94
  66.1 118.1 %copy-start.3 = (bf16[32,40,256]{2,1,0:T(8,128)(2,1)}, bf16[32,40,256]{2,1,0:T(8,128)(2,1)S(1)}, u32[]{:S(2)}) copy-start(bf16[32,40,256]{2,1,0:T(8,128)(2,1)S(1)} %all-to-all-done.2) | copy-start | bytes 1966084
  214.1 138.3 %all-gather.6.cloned.1.call-start = ((), (), s32[]{:S(2)}) async-start(), calls=%async_computation.7 | async-start | bytes 2088960 | tf_op jit(solution)/shard_map/all_gather | solution.py:116
  214.8 209.8 %all-gather.8.cloned.1.call-start = ((), (), s32[]{:S(2)}) async-start(), calls=%async_computation.8 | async-start | bytes 2088960 | tf_op jit(solution)/shard_map/all_gather | solution.py:117
  282.4 158.8 %all-to-all-start.1 = ((bf16[32,40,256]{2,1,0:T(8,128)(2,1)}), bf16[32,40,256]{2,1,0:T(8,128)(2,1)S(1)}, u32[]{:S(2)}, u32[]{:S(2)}) async-start(bf16[32,40,256]{2,1,0:T(8,128)(2,1)} %bitcast.7), calls=%async_computation.1 | async-start | bytes 1310720 | tf_op jit(solution)/shard_map/all_to_all | solution.py:98
  355.4 82.8 %collective-permute-start = (bf16[256,768]{1,0:T(8,128)(2,1)}, bf16[256,768]{1,0:T(8,128)(2,1)}, u32[]{:S(2)}, u32[]{:S(2)}) collective-permute-start(bf16[256,768]{1,0:T(8,128)(2,1)} %get-tuple-element.8), channel_id=1, source_target_pairs={{0,16},{1,17},{2,18},{3,19},{4,20},{5,21},{6,22},{7,23},{8,24},{9,... | collective-permute-start | bytes 1179656 | tf_op jit(solution)/shard_map/ppermute | solution.py:10
  424.7 7.2 %copy-start.4 = (bf16[32,40,256]{2,1,0:T(8,128)(2,1)S(1)}, bf16[32,40,256]{2,1,0:T(8,128)(2,1)}, u32[]{:S(2)}) copy-start(bf16[32,40,256]{2,1,0:T(8,128)(2,1)} %copy-done.3) | copy-start | bytes 1966084
  424.7 7.2 %copy-start.13 = (bf16[1280,768]{1,0:T(8,128)(2,1)S(1)}, bf16[1280,768]{1,0:T(8,128)(2,1)}, u32[]{:S(2)}) copy-start(bf16[1280,768]{1,0:T(8,128)(2,1)} %all-gather.4.cloned.1.call-done) | copy-start | bytes 5898244
  427.1 8.8 %copy-start.1 = (bf16[1280,768]{1,0:T(8,128)(2,1)S(1)}, bf16[1280,768]{1,0:T(8,128)(2,1)}, u32[]{:S(2)}) copy-start(bf16[1280,768]{1,0:T(8,128)(2,1)} %all-gather.6.cloned.1.call-done) | copy-start | bytes 5898244
  427.1 13.1 %collective-permute-start.1 = (bf16[256,768]{1,0:T(8,128)(2,1)S(1)}, bf16[256,768]{1,0:T(8,128)(2,1)S(1)}, u32[]{:S(2)}, u32[]{:S(2)}) collective-permute-start(bf16[256,768]{1,0:T(8,128)(2,1)S(1)} %get-tuple-element.10), channel_id=1, source_target_pairs={{0,16},{1,17},{2,18},{3,19},{4,20},{5,21},{6,22},{7,23},{8,24},{9,... | collective-permute-start | bytes 1179656 | tf_op jit(solution)/shard_map/ppermute | solution.py:10
  433.6 3.0 copy-start.2
  433.6 3.0 copy-start.7
  433.6 25.5 %collective-permute-start.2 = (bf16[768,256]{1,0:T(8,128)(2,1)}, bf16[768,256]{1,0:T(8,128)(2,1)}, u32[]{:S(2)}, u32[]{:S(2)}) collective-permute-start(bf16[768,256]{1,0:T(8,128)(2,1)} %get-tuple-element.12), channel_id=1, source_target_pairs={{0,16},{1,17},{2,18},{3,19},{4,20},{5,21},{6,22},{7,23},{8,24},{9,... | collective-permute-start | bytes 1179656 | tf_op jit(solution)/shard_map/ppermute | solution.py:10
  440.2 19.0 %copy-start.8 = (f32[768,256]{1,0:T(8,128)S(1)}, f32[768,256]{1,0:T(8,128)}, u32[]{:S(2)}) copy-start(f32[768,256]{1,0:T(8,128)} %get-tuple-element.13) | copy-start | bytes 2359300
  441.1 30.9 %all-to-all-start.4 = ((bf16[32,40,256]{2,1,0:T(8,128)(2,1)}), bf16[32,40,256]{2,1,0:T(8,128)(2,1)}, u32[]{:S(2)}, u32[]{:S(2)}) async-start(bf16[32,40,256]{2,1,0:T(8,128)(2,1)} %bitcast.13), calls=%async_computation.4 | async-start | bytes 1310720 | tf_op jit(solution)/shard_map/all_to_all | solution.py:125
  461.1 11.0 %copy-start.10 = (pred[1280,128]{1,0:T(8,128)(4,1)S(1)}, pred[1280,128]{1,0:T(8,128)(4,1)}, u32[]{:S(2)}) copy-start(pred[1280,128]{1,0:T(8,128)(4,1)} %copy-done.9) | copy-start | bytes 491524
Sparse Core Ops, SparseCore 0:
  63.1 149.0 reduce-scatter.3
  214.5 64.7 all-gather.3
  282.1 70.2 all-gather.5
  355.2 69.4 all-gather.7
where the time goes:
time: 482 us; the launch traced here: 481 us
  waiting for transfers between devices  226 us (47%)
  blocking collectives  117 us (24%)
  starting transfers between devices  62 us (13%)
  other arithmetic  30.5 us (6%)
  matrix products  22 us (5%)
  between operations  14.7 us (3%)
  local copies, waits for them, and re-layouts  7.99 us (2%)
    all_to_all x1, blocking collectives, per_device(): lax.all_to_all(hidden_parts, 'dp', split_axis=0, concat_axis=0, tiled=True)  117 us
    all_gather x1, waiting for transfers between devices, per_device(): piece_up = lax.all_gather(grad_up_rows, 'dp', axis=0, tiled=True)  64.6 us
    all_gather x1, waiting for transfers between devices, per_device(): piece = lax.all_gather(hid_own, 'dp', axis=0, tiled=True)  56.5 us
    all_gather x1, waiting for transfers between devices, per_device(): piece_gate = lax.all_gather(grad_gate_rows, 'dp', axis=0, tiled=True)  52.7 us
    reduce_scatter x1, waiting for transfers between devices, per_device(): lax.psum_scatter(rounded(jnp.concatenate([product(block_rows, gate_slab),...  27.7 us
    all_to_all x1, starting transfers between devices, per_device(): lax.all_to_all(back_slab.reshape(n_expert, capacity, slab), 'expert', spl...  18 us
    all_to_all x1, starting transfers between devices, per_device(): lax.all_to_all(answer_slab.reshape(n_expert, capacity, slab), 'expert', s...  17.4 us
    ppermute x3, starting transfers between devices, swapped(): return lax.ppermute(value, axis, pairs)  11.7 us
  transfers between devices with their start and end apart: 11, of which 7 were waited for; matrix products, arithmetic and copies ran while one was open for 8% of the time, Pallas kernels for 0%

commit v1 on v0

--- a/solution.py
+++ b/solution.py
@@ -1,7 +1,35 @@
+import functools
 import jax
 import jax.numpy as jnp
 from jax import lax
 from jax.sharding import PartitionSpec as P
+
+
+def derive_lines_in(page, row_dim):
+    g_now = list(page.shape[1:])
+    g_now[row_dim] *= page.shape[0]
+    return jnp.moveaxis(page, 0, row_dim).reshape(g_now)
+
+
+def assign_classes(matrix, axis_name, which_dim):
+    dev_n = lax.axis_size(axis_name)
+    in_order = list(map(lambda m: (m, (m + 1) % dev_n), range(dev_n)))
+    arrivals = [(dev, jj) for jj, dev in in_order]
+    outcome_arr, prior = ([], [])
+    for rr in range(dev_n - 1):
+        if rr % 2 == 0:
+            outcome_arr.append(
+                lax.ppermute(outcome_arr[-1] if outcome_arr else matrix, axis_name, in_order)
+            )
+        else:
+            prior.append(lax.ppermute(prior[-1] if prior else matrix, axis_name, arrivals))
+    arr_out = jnp.stack([*outcome_arr[::-1], matrix, *prior])
+    moved = lax.axis_index(axis_name) - len(outcome_arr)
+    arr_out = arr_out[(jnp.arange(dev_n) - moved) % dev_n]
+    return derive_lines_in(arr_out, which_dim)
+
+
+_push_records = functools.partial(assign_classes, axis_name="dp", which_dim=0)
 
 
 def swapped(value, axis, stride):
@@ -114,7 +142,7 @@
     )
     grad_up_rows = (grad_hidden * activated).astype(jnp.bfloat16)
     piece_gate = lax.all_gather(grad_gate_rows, "dp", axis=0, tiled=True)
-    piece_up = lax.all_gather(grad_up_rows, "dp", axis=0, tiled=True)
+    piece_up = _push_records(grad_up_rows)
     block_rows = token_slab
     gate_acc = inner_rows(block_rows, piece_gate)
     up_acc = inner_rows(block_rows, piece_up)

time: 482 us -> 401 us (0.83)
  waiting for transfers between devices: 226 us -> 82.1 us
  starting transfers between devices: 62 us -> 111 us
  local copies, waits for them, and re-layouts: 7.99 us -> 20.7 us
    all_gather x1 -> x0, waiting for transfers between devices: 64.6 us -> none  [per_device(): piece_up = lax.all_gather(grad_up_rows, 'dp', axis=0, tiled=True)]
    all_gather x1, waiting for transfers between devices: 52.7 us -> 0.01 us  [per_device(): piece_gate = lax.all_gather(grad_gate_rows, 'dp', axis=0, tiled=True)]
    ppermute x0 -> x15, starting transfers between devices: none -> 49.4 us  [the longest x7 32.9 us: assign_classes(): lax.ppermute(prior[-1] if prior else matrix, axis_name, arrivals)]
    all_gather x1, waiting for transfers between devices: 56.5 us -> 21.1 us  [per_device(): piece = lax.all_gather(hid_own, 'dp', axis=0, tiled=True)]
    ppermute x0 -> x15, waiting for transfers between devices: none -> 12.6 us  [the longest x8 11.2 us: assign_classes(): lax.ppermute(outcome_arr[-1] if outcome_arr else matrix, axis_name, in_or...]
    unnamed x31 -> x42, local copies, waits for them, and re-layouts: 7.29 us -> 17.2 us
    all_to_all x1, waiting for transfers between devices: 9.76 us -> 0.01 us  [per_device(): lax.all_to_all(back_slab.reshape(n_expert, capacity, slab), 'expert', spl...]
    all_to_all x1, waiting for transfers between devices: 0.01 us -> 6.78 us  [per_device(): lax.all_to_all(answer_slab.reshape(n_expert, capacity, slab), 'expert', s...]
  transfers between devices with their start and end apart: 11 -> 25, of which waited for: 7 -> 16; matrix products, arithmetic and copies ran while one was open for 8% -> 13% of each run, Pallas kernels for 0% -> 0%
where the time goes in v1:
time: 401 us; the launch traced here: 399 us
  blocking collectives  117 us (29%)
  starting transfers between devices  111 us (28%)
  waiting for transfers between devices  82.1 us (20%)
  other arithmetic  31.4 us (8%)
  matrix products  21.8 us (5%)
  local copies, waits for them, and re-layouts  20.7 us (5%)
  between operations  14.9 us (4%)
    all_to_all x1, blocking collectives, per_device(): lax.all_to_all(hidden_parts, 'dp', split_axis=0, concat_axis=0, tiled=True)  117 us
    ppermute x7, starting transfers between devices, assign_classes(): lax.ppermute(prior[-1] if prior else matrix, axis_name, arrivals)  32.9 us
    reduce_scatter x1, waiting for transfers between devices, per_device(): lax.psum_scatter(rounded(jnp.concatenate([product(block_rows, gate_slab),...  27.7 us
    all_gather x1, waiting for transfers between devices, per_device(): piece = lax.all_gather(hid_own, 'dp', axis=0, tiled=True)  21.1 us
    all_to_all x1, starting transfers between devices, per_device(): lax.all_to_all(back_slab.reshape(n_expert, capacity, slab), 'expert', spl...  19 us
    unnamed x42, local copies, waits for them, and re-layouts  17.2 us
    ppermute x8, starting transfers between devices, assign_classes(): lax.ppermute(outcome_arr[-1] if outcome_arr else matrix, axis_name, in_or...  16.5 us
    all_to_all x1, starting transfers between devices, per_device(): lax.all_to_all(answer_slab.reshape(n_expert, capacity, slab), 'expert', s...  15.1 us
  transfers between devices with their start and end apart: 25, of which 16 were waited for; matrix products, arithmetic and copies ran while one was open for 13% of the time, Pallas kernels for 0%

profile of v1, /device:TPU:1, one launch (start us, length us, event | category | flops | bytes accessed | tf_op | source)
XLA Modules:
  0.0 399.5 jit_solution(3356113379425192773)
XLA Ops:
  7.2 0.8 copy.42
  8.2 9.0 %reduce-window.6 = s32[32,8,128]{2,1,0:T(8,128)S(1)} reduce-window(s32[32,8,128]{2,1,0:T(8,128)S(1)} %fusion.24, s32[]{:T(128)} %constant.33.clone.1), window={size=1x1x128 pad=0_0x0_0x127_0}, to_apply=%region_0.0 | reduce-window | flops 4161536 | bytes 262148 | tf_op jit(solution)/shard_map/reduce-window
  17.9 0.7 multiply_add_fusion.1
  18.6 4.6 %fusion = pred[1280,128]{1,0:T(8,128)(4,1)S(1)} fusion(s32[128,8]{0,1:T(8,128)S(1)} %multiply_add_fusion.1), kind=kLoop, calls=%fused_computation.4 | loop fusion | flops 2457600 | bytes 167936 | tf_op jit(solution)/shard_map/reduce_or | solution.py:81
  23.3 2.1 convolution_convert_fusion.4
  25.3 10.4 %all-to-all-start = ((bf16[32,40,256]{2,1,0:T(8,128)(2,1)}), bf16[32,40,256]{2,1,0:T(8,128)(2,1)S(1)}, u32[]{:S(2)}, u32[]{:S(2)}) async-start(bf16[32,40,256]{2,1,0:T(8,128)(2,1)} %bitcast.2), calls=%async_computation | async-start | bytes 1310720 | tf_op jit(solution)/shard_map/all_to_all | solution.py:93
  36.0 1.9 fusion.4
  38.0 10.8 %all-to-all-done = bf16[32,40,256]{2,1,0:T(8,128)(2,1)S(1)} async-done(((bf16[32,40,256]{2,1,0:T(8,128)(2,1)}), bf16[32,40,256]{2,1,0:T(8,128)(2,1)S(1)}, u32[]{:S(2)}, u32[]{:S(2)}) %all-to-all-start) | async-done | bytes 655392 | tf_op jit(solution)/shard_map/all_to_all | solution.py:93
  48.8 4.1 %all-to-all-start.2 = ((bf16[32,40,256]{2,1,0:T(8,128)(2,1)}), bf16[32,40,256]{2,1,0:T(8,128)(2,1)S(1)}, u32[]{:S(2)}, u32[]{:S(2)}) async-start(bf16[32,40,256]{2,1,0:T(8,128)(2,1)} %bitcast.10), calls=%async_computation.2 | async-start | bytes 1310720 | tf_op jit(solution)/shard_map/all_to_all | solution.py:100
  53.0 0.7 convolution_convert_fusion.1
  53.7 0.7 convolution_convert_fusion.2
  54.4 2.2 pad_maximum_fusion
  56.6 6.3 %copy.49 = bf16[1280,1536]{1,0:T(8,128)(2,1)} copy(bf16[1280,1536]{0,1:T(8,128)(2,1)} %pad_maximum_fusion) | data formatting | bytes 7864320
  62.9 3.0 all-to-all-done.2
  65.9 0.7 convolution_convert_fusion
  66.6 117.4 %all_to_all.25 = bf16[16,80,768]{2,1,0:T(8,128)(2,1)S(1)} all-to-all(bf16[16,80,768]{2,1,0:T(8,128)(2,1)S(1)} %bitcast.114), channel_id=1, replica_groups=mesh['dp'=16,'expert'=32] {'dp'}, dimensions={0} | all-to-all | bytes 3932160 | tf_op jit(solution)/shard_map/all_to_all | solution.py:136
  184.3 27.7 %reduce-scatter.4.cloned.1.call-done = bf16[80,1536]{1,0:T(8,128)(2,1)} async-done(((bf16[1280,1536]{1,0:T(8,128)(2,1)}), bf16[80,1536]{1,0:T(8,128)(2,1)}) %reduce-scatter.4.cloned.1.call-update) | async-done | bytes 245776 | tf_op jit(solution)/shard_map/reduce_scatter | solution.py:111
  212.0 1.0 convert_element_type.90
  212.9 0.8 multiply_convert_fusion
  213.8 3.1 collective-permute-start
  217.0 3.7 collective-permute-done
  220.7 1.9 collective-permute-start.1
  222.6 4.6 %collective-permute-start.8 = (bf16[80,768]{1,0:T(8,128)(2,1)S(1)}, bf16[80,768]{1,0:T(8,128)(2,1)S(1)}, u32[]{:S(2)}, u32[]{:S(2)}) collective-permute-start(bf16[80,768]{1,0:T(8,128)(2,1)S(1)} %get-tuple-element.5), channel_id=1, source_target_pairs={{32,0},{64,32},{96,64},{128,96},{160,128},{192,160},{224,192},{256... | collective-permute-start | bytes 368648 | tf_op jit(solution)/shard_map/ppermute | solution.py:25
  227.2 0.7 collective-permute-done.1
  227.9 1.9 collective-permute-start.2
  229.8 4.6 %collective-permute-start.9 = (bf16[80,768]{1,0:T(8,128)(2,1)S(1)}, bf16[80,768]{1,0:T(8,128)(2,1)S(1)}, u32[]{:S(2)}, u32[]{:S(2)}) collective-permute-start(bf16[80,768]{1,0:T(8,128)(2,1)S(1)} %collective-permute-done.8), channel_id=1, source_target_pairs={{32,0},{64,32},{96,64},{128,96},{160,128},{192,160},{224,192},{256... | collective-permute-start | bytes 368648 | tf_op jit(solution)/shard_map/ppermute | solution.py:25
  234.4 1.7 collective-permute-done.2
  236.1 1.9 collective-permute-start.3
  238.0 5.3 %collective-permute-start.10 = (bf16[80,768]{1,0:T(8,128)(2,1)S(1)}, bf16[80,768]{1,0:T(8,128)(2,1)S(1)}, u32[]{:S(2)}, u32[]{:S(2)}) collective-permute-start(bf16[80,768]{1,0:T(8,128)(2,1)S(1)} %collective-permute-done.9), channel_id=1, source_target_pairs={{32,0},{64,32},{96,64},{128,96},{160,128},{192,160},{224,192},{256... | collective-permute-start | bytes 368648 | tf_op jit(solution)/shard_map/ppermute | solution.py:25
  243.3 1.9 collective-permute-done.3
  245.2 1.9 collective-permute-start.4
  247.1 5.2 %collective-permute-start.11 = (bf16[80,768]{1,0:T(8,128)(2,1)S(1)}, bf16[80,768]{1,0:T(8,128)(2,1)S(1)}, u32[]{:S(2)}, u32[]{:S(2)}) collective-permute-start(bf16[80,768]{1,0:T(8,128)(2,1)S(1)} %collective-permute-done.10), channel_id=1, source_target_pairs={{32,0},{64,32},{96,64},{128,96},{160,128},{192,160},{224,192},{256... | collective-permute-start | bytes 368648 | tf_op jit(solution)/shard_map/ppermute | solution.py:25
  252.7 2.0 collective-permute-start.5
  255.1 4.6 %collective-permute-start.12 = (bf16[80,768]{1,0:T(8,128)(2,1)S(1)}, bf16[80,768]{1,0:T(8,128)(2,1)S(1)}, u32[]{:S(2)}, u32[]{:S(2)}) collective-permute-start(bf16[80,768]{1,0:T(8,128)(2,1)S(1)} %collective-permute-done.11), channel_id=1, source_target_pairs={{32,0},{64,32},{96,64},{128,96},{160,128},{192,160},{224,192},{256... | collective-permute-start | bytes 368648 | tf_op jit(solution)/shard_map/ppermute | solution.py:25
  260.2 1.9 collective-permute-start.6
  262.2 0.7 collective-permute-done.12
  262.8 4.4 %collective-permute-start.13 = (bf16[80,768]{1,0:T(8,128)(2,1)S(1)}, bf16[80,768]{1,0:T(8,128)(2,1)S(1)}, u32[]{:S(2)}, u32[]{:S(2)}) collective-permute-start(bf16[80,768]{1,0:T(8,128)(2,1)S(1)} %collective-permute-done.12), channel_id=1, source_target_pairs={{32,0},{64,32},{96,64},{128,96},{160,128},{192,160},{224,192},{256... | collective-permute-start | bytes 368648 | tf_op jit(solution)/shard_map/ppermute | solution.py:25
  267.2 0.9 collective-permute-done.6
  268.1 1.9 collective-permute-start.7
  270.4 4.4 %collective-permute-start.14 = (bf16[80,768]{1,0:T(8,128)(2,1)S(1)}, bf16[80,768]{1,0:T(8,128)(2,1)S(1)}, u32[]{:S(2)}, u32[]{:S(2)}) collective-permute-start(bf16[80,768]{1,0:T(8,128)(2,1)S(1)} %collective-permute-done.13), channel_id=1, source_target_pairs={{32,0},{64,32},{96,64},{128,96},{160,128},{192,160},{224,192},{256... | collective-permute-start | bytes 368648 | tf_op jit(solution)/shard_map/ppermute | solution.py:25
  274.8 1.3 collective-permute-done.7
  276.1 0.7 bitcast_dynamic-update-slice_fusion.15
  278.7 0.7 bitcast_dynamic-update-slice_fusion.11
  282.0 0.7 bitcast_dynamic-update-slice_fusion.6
  286.6 2.2 gather_fusion
  288.9 0.7 fusion.28
  289.6 3.9 collective-permute-start.16
  294.1 7.6 %select_reduce_fusion = f32[1280,128]{1,0:T(8,128)} fusion(f32[128,8]{0,1:T(8,128)S(1)} %copy-done.10, s32[128,8]{0,1:T(8,128)S(1)} %multiply_add_fusion.1), kind=kLoop, calls=%fused_computation.2 | loop fusion | flops 3768320 | bytes 663552 | tf_op jit(solution)/shard_map/reduce_sum | solution.py:82
  301.7 1.0 add_bitcast_fusion.1
  302.7 2.3 fusion.14
  304.9 1.6 fusion.3
  306.5 19.0 %all-to-all-start.4 = ((bf16[32,40,256]{2,1,0:T(8,128)(2,1)}), bf16[32,40,256]{2,1,0:T(8,128)(2,1)}, u32[]{:S(2)}, u32[]{:S(2)}) async-start(bf16[32,40,256]{2,1,0:T(8,128)(2,1)} %bitcast.119), calls=%async_computation.4 | async-start | bytes 1310720 | tf_op jit(solution)/shard_map/all_to_all | solution.py:153
  325.5 3.1 fusion.27
  328.5 4.9 %collective-permute-start.15 = (bf16[256,768]{1,0:T(8,128)(2,1)}, bf16[256,768]{1,0:T(8,128)(2,1)}, u32[]{:S(2)}, u32[]{:S(2)}) collective-permute-start(bf16[256,768]{1,0:T(8,128)(2,1)} %get-tuple-element.8), channel_id=1, source_target_pairs={{0,16},{1,17},{2,18},{3,19},{4,20},{5,21},{6,22},{7,23},{8,24},{9,... | collective-permute-start | bytes 1179656 | tf_op jit(solution)/shard_map/ppermute | solution.py:38
  333.5 21.1 %all-gather.3.cloned.1.call-done = bf16[1280,768]{1,0:T(8,128)(2,1)} async-done(((bf16[80,768]{1,0:T(8,128)(2,1)}), bf16[1280,768]{1,0:T(8,128)(2,1)}) %all-gather.3.cloned.1.call-update) | async-done | bytes 1966096 | tf_op jit(solution)/shard_map/all_gather | solution.py:122
  354.6 3.2 fusion.29
  357.8 4.3 %collective-permute-start.17 = (bf16[768,256]{1,0:T(8,128)(2,1)}, bf16[768,256]{1,0:T(8,128)(2,1)}, u32[]{:S(2)}, u32[]{:S(2)}) collective-permute-start(bf16[768,256]{1,0:T(8,128)(2,1)} %get-tuple-element.12), channel_id=1, source_target_pairs={{0,16},{1,17},{2,18},{3,19},{4,20},{5,21},{6,22},{7,23},{8,24},{9,... | collective-permute-start | bytes 1179656 | tf_op jit(solution)/shard_map/ppermute | solution.py:38
  362.1 1.5 convolution_convert_fusion.3
  363.7 15.1 %all-to-all-start.1 = ((bf16[32,40,256]{2,1,0:T(8,128)(2,1)}), bf16[32,40,256]{2,1,0:T(8,128)(2,1)S(1)}, u32[]{:S(2)}, u32[]{:S(2)}) async-start(bf16[32,40,256]{2,1,0:T(8,128)(2,1)} %bitcast.7), calls=%async_computation.1 | async-start | bytes 1310720 | tf_op jit(solution)/shard_map/all_to_all | solution.py:126
  378.8 2.0 add_bitcast_fusion.2
  380.9 2.0 add_bitcast_fusion
  382.8 2.1 convolution_convert_fusion.5
  384.9 6.8 %all-to-all-done.1 = bf16[32,40,256]{2,1,0:T(8,128)(2,1)S(1)} async-done(((bf16[32,40,256]{2,1,0:T(8,128)(2,1)}), bf16[32,40,256]{2,1,0:T(8,128)(2,1)S(1)}, u32[]{:S(2)}, u32[]{:S(2)}) %all-to-all-start.1) | async-done | bytes 655392 | tf_op jit(solution)/shard_map/all_to_all | solution.py:126
  392.0 0.9 fusion.5
  (76 shorter events, 12.1 us)
Async XLA Ops:
  7.2 46.5 %copy-start = (bf16[1,256,768]{2,1,0:T(8,128)(2,1)S(1)}, bf16[1,256,768]{2,1,0:T(8,128)(2,1)}, u32[]{:S(2)}) copy-start(bf16[1,256,768]{2,1,0:T(8,128)(2,1)} %param.12) | copy-start | bytes 1179652
  8.0 27.8 %copy-start.9 = (bf16[128,256]{1,0:T(8,128)(2,1)S(1)}, bf16[128,256]{1,0:T(8,128)(2,1)}, u32[]{:S(2)}) copy-start(bf16[128,256]{1,0:T(8,128)(2,1)} %param.15) | copy-start | bytes 196612
  8.2 27.6 %copy-start.10 = (f32[128,8]{0,1:T(8,128)S(1)}, f32[128,8]{0,1:T(8,128)}, u32[]{:S(2)}) copy-start(f32[128,8]{0,1:T(8,128)} %param.10) | copy-start | bytes 12292
  23.3 2.1 copy-start.5
  25.3 23.5 %all-to-all-start = ((bf16[32,40,256]{2,1,0:T(8,128)(2,1)}), bf16[32,40,256]{2,1,0:T(8,128)(2,1)S(1)}, u32[]{:S(2)}, u32[]{:S(2)}) async-start(bf16[32,40,256]{2,1,0:T(8,128)(2,1)} %bitcast.2), calls=%async_computation | async-start | bytes 1310720 | tf_op jit(solution)/shard_map/all_to_all | solution.py:93
  36.0 16.9 %copy-start.4 = (bf16[1,256,768]{2,1,0:T(8,128)(2,1)S(1)}, bf16[1,256,768]{2,1,0:T(8,128)(2,1)}, u32[]{:S(2)}) copy-start(bf16[1,256,768]{2,1,0:T(8,128)(2,1)} %param.13) | copy-start | bytes 1179652
  48.8 17.1 %all-to-all-start.2 = ((bf16[32,40,256]{2,1,0:T(8,128)(2,1)}), bf16[32,40,256]{2,1,0:T(8,128)(2,1)S(1)}, u32[]{:S(2)}, u32[]{:S(2)}) async-start(bf16[32,40,256]{2,1,0:T(8,128)(2,1)} %bitcast.10), calls=%async_computation.2 | async-start | bytes 1310720 | tf_op jit(solution)/shard_map/all_to_all | solution.py:100
  52.9 159.1 %reduce-scatter.4.cloned.1.call-start = ((), (), s32[]{:S(2)}) async-start(), calls=%async_computation.8 | async-start | bytes 4177920 | tf_op jit(solution)/shard_map/reduce_scatter | solution.py:111
  62.8 3.1 copy-start.7
  62.9 239.8 %all-gather.5.cloned.1.call-start = ((), (), s32[]{:S(2)}) async-start(), calls=%async_computation.7 | async-start | bytes 2088960 | tf_op jit(solution)/shard_map/all_gather | solution.py:144
  65.9 118.1 %copy-start.2 = (bf16[32,40,256]{2,1,0:T(8,128)(2,1)}, bf16[32,40,256]{2,1,0:T(8,128)(2,1)S(1)}, u32[]{:S(2)}) copy-start(bf16[32,40,256]{2,1,0:T(8,128)(2,1)S(1)} %all-to-all-done.2) | copy-start | bytes 1966084
  213.8 140.8 %all-gather.3.cloned.1.call-start = ((), (), s32[]{:S(2)}) async-start(), calls=%async_computation.6 | async-start | bytes 2088960 | tf_op jit(solution)/shard_map/all_gather | solution.py:122
  213.8 6.8 %collective-permute-start = (bf16[80,768]{1,0:T(8,128)(2,1)S(1)}, bf16[80,768]{1,0:T(8,128)(2,1)S(1)}, u32[]{:S(2)}, u32[]{:S(2)}) collective-permute-start(bf16[80,768]{1,0:T(8,128)(2,1)S(1)} %get-tuple-element.5), channel_id=1, source_target_pairs={{0,32},{32,64},{64,96},{96,128},{128,160},{160,192},{192,224},{224... | collective-permute-start | bytes 368648 | tf_op jit(solution)/shard_map/ppermute | solution.py:22
  220.7 7.2 %collective-permute-start.1 = (bf16[80,768]{1,0:T(8,128)(2,1)S(1)}, bf16[80,768]{1,0:T(8,128)(2,1)S(1)}, u32[]{:S(2)}, u32[]{:S(2)}) collective-permute-start(bf16[80,768]{1,0:T(8,128)(2,1)S(1)} %collective-permute-done), channel_id=1, source_target_pairs={{0,32},{32,64},{64,96},{96,128},{128,160},{160,192},{192,224},{224... | collective-permute-start | bytes 368648 | tf_op jit(solution)/shard_map/ppermute | solution.py:22
  222.6 7.2 %collective-permute-start.8 = (bf16[80,768]{1,0:T(8,128)(2,1)S(1)}, bf16[80,768]{1,0:T(8,128)(2,1)S(1)}, u32[]{:S(2)}, u32[]{:S(2)}) collective-permute-start(bf16[80,768]{1,0:T(8,128)(2,1)S(1)} %get-tuple-element.5), channel_id=1, source_target_pairs={{32,0},{64,32},{96,64},{128,96},{160,128},{192,160},{224,192},{256... | collective-permute-start | bytes 368648 | tf_op jit(solution)/shard_map/ppermute | solution.py:25
  227.9 8.2 %collective-permute-start.2 = (bf16[80,768]{1,0:T(8,128)(2,1)S(1)}, bf16[80,768]{1,0:T(8,128)(2,1)S(1)}, u32[]{:S(2)}, u32[]{:S(2)}) collective-permute-start(bf16[80,768]{1,0:T(8,128)(2,1)S(1)} %collective-permute-done.1), channel_id=1, source_target_pairs={{0,32},{32,64},{64,96},{96,128},{128,160},{160,192},{192,224},{224... | collective-permute-start | bytes 368648 | tf_op jit(solution)/shard_map/ppermute | solution.py:22
  229.8 8.2 %collective-permute-start.9 = (bf16[80,768]{1,0:T(8,128)(2,1)S(1)}, bf16[80,768]{1,0:T(8,128)(2,1)S(1)}, u32[]{:S(2)}, u32[]{:S(2)}) collective-permute-start(bf16[80,768]{1,0:T(8,128)(2,1)S(1)} %collective-permute-done.8), channel_id=1, source_target_pairs={{32,0},{64,32},{96,64},{128,96},{160,128},{192,160},{224,192},{256... | collective-permute-start | bytes 368648 | tf_op jit(solution)/shard_map/ppermute | solution.py:25
  236.1 9.1 %collective-permute-start.3 = (bf16[80,768]{1,0:T(8,128)(2,1)S(1)}, bf16[80,768]{1,0:T(8,128)(2,1)S(1)}, u32[]{:S(2)}, u32[]{:S(2)}) collective-permute-start(bf16[80,768]{1,0:T(8,128)(2,1)S(1)} %collective-permute-done.2), channel_id=1, source_target_pairs={{0,32},{32,64},{64,96},{96,128},{128,160},{160,192},{192,224},{224... | collective-permute-start | bytes 368648 | tf_op jit(solution)/shard_map/ppermute | solution.py:22
  238.0 9.1 %collective-permute-start.10 = (bf16[80,768]{1,0:T(8,128)(2,1)S(1)}, bf16[80,768]{1,0:T(8,128)(2,1)S(1)}, u32[]{:S(2)}, u32[]{:S(2)}) collective-permute-start(bf16[80,768]{1,0:T(8,128)(2,1)S(1)} %collective-permute-done.9), channel_id=1, source_target_pairs={{32,0},{64,32},{96,64},{128,96},{160,128},{192,160},{224,192},{256... | collective-permute-start | bytes 368648 | tf_op jit(solution)/shard_map/ppermute | solution.py:25
  245.2 7.5 %collective-permute-start.4 = (bf16[80,768]{1,0:T(8,128)(2,1)S(1)}, bf16[80,768]{1,0:T(8,128)(2,1)S(1)}, u32[]{:S(2)}, u32[]{:S(2)}) collective-permute-start(bf16[80,768]{1,0:T(8,128)(2,1)S(1)} %collective-permute-done.3), channel_id=1, source_target_pairs={{0,32},{32,64},{64,96},{96,128},{128,160},{160,192},{192,224},{224... | collective-permute-start | bytes 368648 | tf_op jit(solution)/shard_map/ppermute | solution.py:22
  247.1 7.9 %collective-permute-start.11 = (bf16[80,768]{1,0:T(8,128)(2,1)S(1)}, bf16[80,768]{1,0:T(8,128)(2,1)S(1)}, u32[]{:S(2)}, u32[]{:S(2)}) collective-permute-start(bf16[80,768]{1,0:T(8,128)(2,1)S(1)} %collective-permute-done.10), channel_id=1, source_target_pairs={{32,0},{64,32},{96,64},{128,96},{160,128},{192,160},{224,192},{256... | collective-permute-start | bytes 368648 | tf_op jit(solution)/shard_map/ppermute | solution.py:25
  252.7 7.5 %collective-permute-start.5 = (bf16[80,768]{1,0:T(8,128)(2,1)S(1)}, bf16[80,768]{1,0:T(8,128)(2,1)S(1)}, u32[]{:S(2)}, u32[]{:S(2)}) collective-permute-start(bf16[80,768]{1,0:T(8,128)(2,1)S(1)} %collective-permute-done.4), channel_id=1, source_target_pairs={{0,32},{32,64},{64,96},{96,128},{128,160},{160,192},{192,224},{224... | collective-permute-start | bytes 368648 | tf_op jit(solution)/shard_map/ppermute | solution.py:22
  255.1 7.8 %collective-permute-start.12 = (bf16[80,768]{1,0:T(8,128)(2,1)S(1)}, bf16[80,768]{1,0:T(8,128)(2,1)S(1)}, u32[]{:S(2)}, u32[]{:S(2)}) collective-permute-start(bf16[80,768]{1,0:T(8,128)(2,1)S(1)} %collective-permute-done.11), channel_id=1, source_target_pairs={{32,0},{64,32},{96,64},{128,96},{160,128},{192,160},{224,192},{256... | collective-permute-start | bytes 368648 | tf_op jit(solution)/shard_map/ppermute | solution.py:25
  260.2 7.8 %collective-permute-start.6 = (bf16[80,768]{1,0:T(8,128)(2,1)S(1)}, bf16[80,768]{1,0:T(8,128)(2,1)S(1)}, u32[]{:S(2)}, u32[]{:S(2)}) collective-permute-start(bf16[80,768]{1,0:T(8,128)(2,1)S(1)} %collective-permute-done.5), channel_id=1, source_target_pairs={{0,32},{32,64},{64,96},{96,128},{128,160},{160,192},{192,224},{224... | collective-permute-start | bytes 368648 | tf_op jit(solution)/shard_map/ppermute | solution.py:22
  262.8 7.6 %collective-permute-start.13 = (bf16[80,768]{1,0:T(8,128)(2,1)S(1)}, bf16[80,768]{1,0:T(8,128)(2,1)S(1)}, u32[]{:S(2)}, u32[]{:S(2)}) collective-permute-start(bf16[80,768]{1,0:T(8,128)(2,1)S(1)} %collective-permute-done.12), channel_id=1, source_target_pairs={{32,0},{64,32},{96,64},{128,96},{160,128},{192,160},{224,192},{256... | collective-permute-start | bytes 368648 | tf_op jit(solution)/shard_map/ppermute | solution.py:25
  268.1 8.0 %collective-permute-start.7 = (bf16[80,768]{1,0:T(8,128)(2,1)S(1)}, bf16[80,768]{1,0:T(8,128)(2,1)S(1)}, u32[]{:S(2)}, u32[]{:S(2)}) collective-permute-start(bf16[80,768]{1,0:T(8,128)(2,1)S(1)} %collective-permute-done.6), channel_id=1, source_target_pairs={{0,32},{32,64},{64,96},{96,128},{128,160},{160,192},{192,224},{224... | collective-permute-start | bytes 368648 | tf_op jit(solution)/shard_map/ppermute | solution.py:22
  270.4 15.5 %collective-permute-start.14 = (bf16[80,768]{1,0:T(8,128)(2,1)S(1)}, bf16[80,768]{1,0:T(8,128)(2,1)S(1)}, u32[]{:S(2)}, u32[]{:S(2)}) collective-permute-start(bf16[80,768]{1,0:T(8,128)(2,1)S(1)} %collective-permute-done.13), channel_id=1, source_target_pairs={{32,0},{64,32},{96,64},{128,96},{160,128},{192,160},{224,192},{256... | collective-permute-start | bytes 368648 | tf_op jit(solution)/shard_map/ppermute | solution.py:25
  289.6 12.1 %collective-permute-start.16 = (bf16[256,768]{1,0:T(8,128)(2,1)S(1)}, bf16[256,768]{1,0:T(8,128)(2,1)S(1)}, u32[]{:S(2)}, u32[]{:S(2)}) collective-permute-start(bf16[256,768]{1,0:T(8,128)(2,1)S(1)} %get-tuple-element.10), channel_id=1, source_target_pairs={{0,16},{1,17},{2,18},{3,19},{4,20},{5,21},{6,22},{7,23},{8,24},{9,... | collective-permute-start | bytes 1179656 | tf_op jit(solution)/shard_map/ppermute | solution.py:38
  306.5 57.2 %all-to-all-start.4 = ((bf16[32,40,256]{2,1,0:T(8,128)(2,1)}), bf16[32,40,256]{2,1,0:T(8,128)(2,1)}, u32[]{:S(2)}, u32[]{:S(2)}) async-start(bf16[32,40,256]{2,1,0:T(8,128)(2,1)} %bitcast.119), calls=%async_computation.4 | async-start | bytes 1310720 | tf_op jit(solution)/shard_map/all_to_all | solution.py:153
  325.5 29.1 %copy-start.3 = (bf16[32,40,256]{2,1,0:T(8,128)(2,1)S(1)}, bf16[32,40,256]{2,1,0:T(8,128)(2,1)}, u32[]{:S(2)}) copy-start(bf16[32,40,256]{2,1,0:T(8,128)(2,1)} %copy-done.2) | copy-start | bytes 1966084
  328.5 33.6 %copy-start.8 = (bf16[1,768,256]{2,1,0:T(8,128)(2,1)S(1)}, bf16[1,768,256]{2,1,0:T(8,128)(2,1)}, u32[]{:S(2)}) copy-start(bf16[1,768,256]{2,1,0:T(8,128)(2,1)} %param.14) | copy-start | bytes 1179652
  328.5 50.3 %collective-permute-start.15 = (bf16[256,768]{1,0:T(8,128)(2,1)}, bf16[256,768]{1,0:T(8,128)(2,1)}, u32[]{:S(2)}, u32[]{:S(2)}) collective-permute-start(bf16[256,768]{1,0:T(8,128)(2,1)} %get-tuple-element.8), channel_id=1, source_target_pairs={{0,16},{1,17},{2,18},{3,19},{4,20},{5,21},{6,22},{7,23},{8,24},{9,... | collective-permute-start | bytes 1179656 | tf_op jit(solution)/shard_map/ppermute | solution.py:38
  354.6 7.5 %copy-start.11 = (bf16[1280,768]{1,0:T(8,128)(2,1)S(1)}, bf16[1280,768]{1,0:T(8,128)(2,1)}, u32[]{:S(2)}) copy-start(bf16[1280,768]{1,0:T(8,128)(2,1)} %all-gather.3.cloned.1.call-done) | copy-start | bytes 5898244
  357.8 23.1 %collective-permute-start.17 = (bf16[768,256]{1,0:T(8,128)(2,1)}, bf16[768,256]{1,0:T(8,128)(2,1)}, u32[]{:S(2)}, u32[]{:S(2)}) collective-permute-start(bf16[768,256]{1,0:T(8,128)(2,1)} %get-tuple-element.12), channel_id=1, source_target_pairs={{0,16},{1,17},{2,18},{3,19},{4,20},{5,21},{6,22},{7,23},{8,24},{9,... | collective-permute-start | bytes 1179656 | tf_op jit(solution)/shard_map/ppermute | solution.py:38
  363.7 28.1 %all-to-all-start.1 = ((bf16[32,40,256]{2,1,0:T(8,128)(2,1)}), bf16[32,40,256]{2,1,0:T(8,128)(2,1)S(1)}, u32[]{:S(2)}, u32[]{:S(2)}) async-start(bf16[32,40,256]{2,1,0:T(8,128)(2,1)} %bitcast.7), calls=%async_computation.1 | async-start | bytes 1310720 | tf_op jit(solution)/shard_map/all_to_all | solution.py:126
  378.8 4.0 %copy-start.6 = (pred[1280,128]{1,0:T(8,128)(4,1)S(1)}, pred[1280,128]{1,0:T(8,128)(4,1)}, u32[]{:S(2)}) copy-start(pred[1280,128]{1,0:T(8,128)(4,1)} %copy-done.5) | copy-start | bytes 491524
  378.8 12.9 %copy-start.1 = (f32[1280,128]{1,0:T(8,128)S(1)}, f32[1280,128]{1,0:T(8,128)}, u32[]{:S(2)}) copy-start(f32[1280,128]{1,0:T(8,128)} %select_reduce_fusion) | copy-start | bytes 1966084
Sparse Core Ops, SparseCore 0:
  63.0 148.9 reduce-scatter.3
  214.8 69.2 all-gather.4
  286.4 68.0 all-gather.2
